TPU v7x, 32 devices: a whole 2x2x4 slice. The times are simulated.
32 devices in a mesh: dp: 8 (over y, x, core), ctx: 4 (over z).
Axes of the slice: x: 2, y: 2, z: 4, core: 2. Of those that a mesh axis runs over, the one named last changes fastest.
Arguments:
- activations: bfloat16 [8, 512, 2048], P('dp', 'ctx'), may hold values from -6 to 6
- segment_ids: int32 [8, 512], P('dp'), may hold values from 0 to 3, never falling along the last dimension, each value on 1 to 256 neighbouring positions
- ln1_gain: bfloat16 [2048], P(('dp', 'ctx')), may hold values from 0.25 to 1.75
- ln1_bias: bfloat16 [2048], P(('dp', 'ctx')), may hold values from -3 to 3
- q_weight: bfloat16 [2048, 2048], P(('dp', 'ctx')), may hold values from -0.125 to 0.125
- q_bias: bfloat16 [2048], P(('dp', 'ctx')), may hold values from -3 to 3
- kv_weight: bfloat16 [2048, 256], P(('dp', 'ctx')), may hold values from -0.125 to 0.125
- v_bias: bfloat16 [128], P(('dp', 'ctx')), may hold values from -3 to 3
- out_weight: bfloat16 [2048, 2048], P(('dp', 'ctx')), may hold values from -1 to 1
- out_bias: bfloat16 [2048], P(('dp', 'ctx')), may hold values from -3 to 3
- ln2_gain: bfloat16 [2048], P(('dp', 'ctx')), may hold values from 0.25 to 1.75
- ln2_bias: bfloat16 [2048], P(('dp', 'ctx')), may hold values from -3 to 3
- up_weight: bfloat16 [2048, 8192], P(('dp', 'ctx')), may hold values from -0.125 to 0.125
- up_bias: bfloat16 [8192], P(('dp', 'ctx')), may hold values from -3 to 3
- down_weight: bfloat16 [8192, 2048], P(('dp', 'ctx')), may hold values from -0.0625 to 0.0625
- down_bias: bfloat16 [2048], P(('dp', 'ctx')), may hold values from -3 to 3
- cotangent: bfloat16 [8, 512, 2048], P('dp', 'ctx'), may hold values from -6 to 6
Outputs:
- output: bfloat16 [8, 512, 2048], P('dp', 'ctx')
- input_grad: bfloat16 [8, 512, 2048], P('dp', 'ctx')
- ln1_gain_grad: float32 [2048], P(('dp', 'ctx'))
- ln1_bias_grad: float32 [2048], P(('dp', 'ctx'))
- q_weight_grad: float32 [2048, 2048], P(('dp', 'ctx'))
- q_bias_grad: float32 [2048], P(('dp', 'ctx'))
- kv_weight_grad: float32 [2048, 256], P(('dp', 'ctx'))
- v_bias_grad: float32 [128], P(('dp', 'ctx'))
- out_weight_grad: float32 [2048, 2048], P(('dp', 'ctx'))
- out_bias_grad: float32 [2048], P(('dp', 'ctx'))
- ln2_gain_grad: float32 [2048], P(('dp', 'ctx'))
- ln2_bias_grad: float32 [2048], P(('dp', 'ctx'))
- up_weight_grad: float32 [2048, 8192], P(('dp', 'ctx'))
- up_bias_grad: float32 [8192], P(('dp', 'ctx'))
- down_weight_grad: float32 [8192, 2048], P(('dp', 'ctx'))
- down_bias_grad: float32 [2048], P(('dp', 'ctx'))
Inputs may be any that keep to these rules, and one draw needn't show every extreme that they name: segment_ids of a row never fall; every one of the 4 documents of a row holds 1 to 256 tokens, and one holds exactly 256.
All inputs are finite; a program needn't handle non-finite values.
Results may differ from a plain program's by a relative error of at most 0.013.
Values may be sent and summed in bfloat16 or wider, within the bound.
No kernel may reach another device: no remote copies, remote signals or barrier semaphores. Data moves between devices by JAX's collectives and lax.ppermute only.
A program may use at most 320 MiB of HBM per device.

v0:
```python
import jax
import jax.numpy as jnp
from jax import lax
from jax.sharding import PartitionSpec as P

HEADS = 16
HD = 128
epsilon = 1e-05


def norm_rows(values, gain, shift):
    center = jnp.mean(values, axis=-1, keepdims=True)
    centered = values - center
    variance = jnp.mean(centered * centered, axis=-1, keepdims=True)
    return centered * lax.rsqrt(variance + epsilon) * gain + shift


def gelu_tanh(values):
    return jax.nn.gelu(values, approximate=True)


def local(
    activations,
    segment_ids,
    ln1_gain,
    ln1_bias,
    q_weight,
    q_bias,
    kv_weight,
    v_bias,
    out_weight,
    out_bias,
    ln2_gain,
    ln2_bias,
    up_weight,
    up_bias,
    down_weight,
    down_bias,
    cotangent,
):
    row_input = activations[0].astype(jnp.float32)
    tokens_here = row_input.shape[0]
    block_index = lax.axis_index("ctx")
    row_segments = segment_ids[0]
    attn_full = (
        lax.all_gather(ln1_gain, ("dp", "ctx"), axis=0, tiled=True),
        lax.all_gather(ln1_bias, ("dp", "ctx"), axis=0, tiled=True),
        lax.all_gather(q_weight, ("dp", "ctx"), axis=0, tiled=True),
        lax.all_gather(q_bias, ("dp", "ctx"), axis=0, tiled=True),
        lax.all_gather(kv_weight, ("dp", "ctx"), axis=0, tiled=True),
        lax.all_gather(v_bias, ("dp", "ctx"), axis=0, tiled=True),
        lax.all_gather(out_weight, ("dp", "ctx"), axis=0, tiled=True),
        lax.all_gather(out_bias, ("dp", "ctx"), axis=0, tiled=True),
    )
    gain_one, shift_one, weight_query, bias_query, weight_kv, bias_value, weight_out, bias_out = (
        attn_full
    )
    normed_one, norm_back_one = jax.vjp(
        norm_rows, row_input, gain_one.astype(jnp.float32), shift_one.astype(jnp.float32)
    )
    hidden_one = normed_one.astype(jnp.bfloat16)
    query_low = (
        jnp.dot(hidden_one, weight_query, preferred_element_type=jnp.float32)
        + bias_query.astype(jnp.float32)
    ).astype(jnp.bfloat16)
    kv_shift = jnp.concatenate([jnp.zeros((HD,), jnp.float32), bias_value.astype(jnp.float32)])
    kv_low = (jnp.dot(hidden_one, weight_kv, preferred_element_type=jnp.float32) + kv_shift).astype(
        jnp.bfloat16
    )
    kv_whole = lax.all_gather(kv_low, "ctx", axis=0, tiled=True)
    key_rows = kv_whole[:, :HD]
    value_rows = kv_whole[:, HD:]
    query_heads = query_low.reshape(tokens_here, HEADS, HD)
    scale_factor = HD ** (-0.5)
    query_start = block_index * tokens_here
    query_places = query_start + jnp.arange(tokens_here, dtype=jnp.int32)
    key_places = jnp.arange(kv_whole.shape[0], dtype=jnp.int32)
    query_segments = lax.dynamic_slice_in_dim(row_segments, query_start, tokens_here)
    allowed = (key_places[None, :] <= query_places[:, None]) & (
        row_segments[None, :] == query_segments[:, None]
    )

    def masked_scores():
        raw_scores = (
            jnp.einsum("thd,jd->htj", query_heads, key_rows, preferred_element_type=jnp.float32)
            * scale_factor
        )
        return jnp.where(allowed[None], raw_scores, -1e30)

    scores = masked_scores()
    biggest = jnp.max(scores, axis=-1, keepdims=True)
    expons = jnp.exp(scores - biggest)
    row_total = jnp.sum(expons, axis=-1, keepdims=True)
    log_total = biggest + jnp.log(row_total)
    soft_low = (expons / row_total).astype(jnp.bfloat16)
    attended = (
        jnp.einsum("htj,jd->thd", soft_low, value_rows, preferred_element_type=jnp.float32)
        .reshape(tokens_here, HEADS * HD)
        .astype(jnp.bfloat16)
    )
    middle = (
        row_input
        + jnp.dot(attended, weight_out, preferred_element_type=jnp.float32)
        + bias_out.astype(jnp.float32)
    )
    mlp_full = (
        lax.all_gather(ln2_gain, ("dp", "ctx"), axis=0, tiled=True),
        lax.all_gather(ln2_bias, ("dp", "ctx"), axis=0, tiled=True),
        lax.all_gather(up_weight, ("dp", "ctx"), axis=0, tiled=True),
        lax.all_gather(up_bias, ("dp", "ctx"), axis=0, tiled=True),
        lax.all_gather(down_weight, ("dp", "ctx"), axis=0, tiled=True),
        lax.all_gather(down_bias, ("dp", "ctx"), axis=0, tiled=True),
    )
    gain_two, shift_two, weight_up, bias_up, weight_down, bias_down = mlp_full
    normed_two, norm_back_two = jax.vjp(
        norm_rows, middle, gain_two.astype(jnp.float32), shift_two.astype(jnp.float32)
    )
    hidden_two = normed_two.astype(jnp.bfloat16)
    preact = jnp.dot(hidden_two, weight_up, preferred_element_type=jnp.float32) + bias_up.astype(
        jnp.float32
    )
    activ_full, gelu_back = jax.vjp(gelu_tanh, preact)
    activ = activ_full.astype(jnp.bfloat16)
    result = (
        middle
        + jnp.dot(activ, weight_down, preferred_element_type=jnp.float32)
        + bias_down.astype(jnp.float32)
    )
    mlp_back = (
        lax.all_gather(ln2_gain, ("dp", "ctx"), axis=0, tiled=True),
        lax.all_gather(ln2_bias, ("dp", "ctx"), axis=0, tiled=True),
        lax.all_gather(up_weight, ("dp", "ctx"), axis=0, tiled=True),
        lax.all_gather(up_bias, ("dp", "ctx"), axis=0, tiled=True),
        lax.all_gather(down_weight, ("dp", "ctx"), axis=0, tiled=True),
        lax.all_gather(down_bias, ("dp", "ctx"), axis=0, tiled=True),
    )
    weight_up_back = mlp_back[2]
    weight_down_back = mlp_back[4]
    grad_low = cotangent[0]
    grad_result = grad_low.astype(jnp.float32)
    grad_activ = jnp.einsum(
        "td,fd->tf", grad_low, weight_down_back, preferred_element_type=jnp.float32
    )
    grad_bias_down = jnp.sum(grad_result, axis=0)
    grad_weight_down = jnp.einsum("tf,td->fd", activ, grad_low, preferred_element_type=jnp.float32)
    down_sums = (
        lax.psum_scatter(grad_weight_down, ("dp", "ctx"), scatter_dimension=0, tiled=True),
        lax.psum_scatter(grad_bias_down, ("dp", "ctx"), scatter_dimension=0, tiled=True),
    )
    grad_preact = gelu_back(grad_activ)[0].astype(jnp.bfloat16)
    grad_bias_up = jnp.sum(grad_preact.astype(jnp.float32), axis=0)
    grad_hidden_two = jnp.einsum(
        "tf,df->td", grad_preact, weight_up_back, preferred_element_type=jnp.float32
    )
    grad_weight_up = jnp.einsum(
        "td,tf->df", hidden_two, grad_preact, preferred_element_type=jnp.float32
    )
    grad_mid_norm, grad_gain_two, grad_shift_two = norm_back_two(grad_hidden_two)
    grad_middle = grad_result + grad_mid_norm
    up_sums = (
        lax.psum_scatter(grad_gain_two, ("dp", "ctx"), scatter_dimension=0, tiled=True),
        lax.psum_scatter(grad_shift_two, ("dp", "ctx"), scatter_dimension=0, tiled=True),
        lax.psum_scatter(grad_weight_up, ("dp", "ctx"), scatter_dimension=0, tiled=True),
        lax.psum_scatter(grad_bias_up, ("dp", "ctx"), scatter_dimension=0, tiled=True),
    )
    attn_back = (
        lax.all_gather(ln1_gain, ("dp", "ctx"), axis=0, tiled=True),
        lax.all_gather(ln1_bias, ("dp", "ctx"), axis=0, tiled=True),
        lax.all_gather(q_weight, ("dp", "ctx"), axis=0, tiled=True),
        lax.all_gather(q_bias, ("dp", "ctx"), axis=0, tiled=True),
        lax.all_gather(kv_weight, ("dp", "ctx"), axis=0, tiled=True),
        lax.all_gather(v_bias, ("dp", "ctx"), axis=0, tiled=True),
        lax.all_gather(out_weight, ("dp", "ctx"), axis=0, tiled=True),
        lax.all_gather(out_bias, ("dp", "ctx"), axis=0, tiled=True),
    )
    weight_query_back = attn_back[2]
    weight_kv_back = attn_back[4]
    weight_out_back = attn_back[6]
    grad_branch = grad_middle.astype(jnp.bfloat16)
    grad_bias_out = jnp.sum(grad_branch.astype(jnp.float32), axis=0)
    grad_weight_out = jnp.einsum(
        "ti,td->id", attended, grad_branch, preferred_element_type=jnp.float32
    )
    grad_attended = (
        jnp.einsum("td,id->ti", grad_branch, weight_out_back, preferred_element_type=jnp.float32)
        .astype(jnp.bfloat16)
        .reshape(tokens_here, HEADS, HD)
    )
    soft_rows = jnp.exp(masked_scores() - log_total)
    soft_again = soft_rows.astype(jnp.bfloat16)
    grad_soft = jnp.einsum(
        "thd,jd->htj", grad_attended, value_rows, preferred_element_type=jnp.float32
    )
    inner_sum = jnp.sum(soft_rows * grad_soft, axis=-1, keepdims=True)
    grad_scores = (soft_rows * (grad_soft - inner_sum)).astype(jnp.bfloat16)
    grad_query = (
        (
            jnp.einsum("htj,jd->thd", grad_scores, key_rows, preferred_element_type=jnp.float32)
            * scale_factor
        )
        .astype(jnp.bfloat16)
        .reshape(tokens_here, HEADS * HD)
    )
    grad_keys = (
        jnp.einsum("htj,thd->jd", grad_scores, query_heads, preferred_element_type=jnp.float32)
        * scale_factor
    )
    grad_values = jnp.einsum(
        "htj,thd->jd", soft_again, grad_attended, preferred_element_type=jnp.float32
    )
    grad_kv_part = jnp.concatenate([grad_keys, grad_values], axis=1)
    grad_kv = lax.psum_scatter(
        grad_kv_part.astype(jnp.bfloat16), "ctx", scatter_dimension=0, tiled=True
    )
    grad_bias_query = jnp.sum(grad_query.astype(jnp.float32), axis=0)
    grad_weight_query = jnp.einsum(
        "td,te->de", hidden_one, grad_query, preferred_element_type=jnp.float32
    )
    grad_bias_value = jnp.sum(grad_kv[:, HD:].astype(jnp.float32), axis=0)
    grad_weight_kv = jnp.einsum(
        "td,te->de", hidden_one, grad_kv, preferred_element_type=jnp.float32
    )
    grad_hidden_one = jnp.einsum(
        "te,de->td", grad_query, weight_query_back, preferred_element_type=jnp.float32
    ) + jnp.einsum("te,de->td", grad_kv, weight_kv_back, preferred_element_type=jnp.float32)
    grad_row_norm, grad_gain_one, grad_shift_one = norm_back_one(grad_hidden_one)
    grad_input = grad_middle + grad_row_norm
    attn_sums = (
        lax.psum_scatter(grad_gain_one, ("dp", "ctx"), scatter_dimension=0, tiled=True),
        lax.psum_scatter(grad_shift_one, ("dp", "ctx"), scatter_dimension=0, tiled=True),
        lax.psum_scatter(grad_weight_query, ("dp", "ctx"), scatter_dimension=0, tiled=True),
        lax.psum_scatter(grad_bias_query, ("dp", "ctx"), scatter_dimension=0, tiled=True),
        lax.psum_scatter(grad_weight_kv, ("dp", "ctx"), scatter_dimension=0, tiled=True),
        lax.psum_scatter(grad_bias_value, ("dp", "ctx"), scatter_dimension=0, tiled=True),
        lax.psum_scatter(grad_weight_out, ("dp", "ctx"), scatter_dimension=0, tiled=True),
        lax.psum_scatter(grad_bias_out, ("dp", "ctx"), scatter_dimension=0, tiled=True),
    )
    return (
        result.astype(jnp.bfloat16)[None],
        grad_input.astype(jnp.bfloat16)[None],
        attn_sums[0],
        attn_sums[1],
        attn_sums[2],
        attn_sums[3],
        attn_sums[4],
        attn_sums[5],
        attn_sums[6],
        attn_sums[7],
        up_sums[0],
        up_sums[1],
        up_sums[2],
        up_sums[3],
        down_sums[0],
        down_sums[1],
    )


def solution(mesh):
    in_specs = (
        P("dp", "ctx", None),
        P("dp", None),
        P(("dp", "ctx")),
        P(("dp", "ctx")),
        P(("dp", "ctx"), None),
        P(("dp", "ctx")),
        P(("dp", "ctx"), None),
        P(("dp", "ctx")),
        P(("dp", "ctx"), None),
        P(("dp", "ctx")),
        P(("dp", "ctx")),
        P(("dp", "ctx")),
        P(("dp", "ctx"), None),
        P(("dp", "ctx")),
        P(("dp", "ctx"), None),
        P(("dp", "ctx")),
        P("dp", "ctx", None),
    )
    out_specs = (
        P("dp", "ctx", None),
        P("dp", "ctx", None),
        P(("dp", "ctx")),
        P(("dp", "ctx")),
        P(("dp", "ctx"), None),
        P(("dp", "ctx")),
        P(("dp", "ctx"), None),
        P(("dp", "ctx")),
        P(("dp", "ctx"), None),
        P(("dp", "ctx")),
        P(("dp", "ctx")),
        P(("dp", "ctx")),
        P(("dp", "ctx"), None),
        P(("dp", "ctx")),
        P(("dp", "ctx"), None),
        P(("dp", "ctx")),
    )
    return jax.shard_map(local, mesh=mesh, in_specs=in_specs, out_specs=out_specs, check_vma=False)
```

profile of v0, /device:TPU:0, one launch (start us, length us, event | category | flops | bytes accessed | tf_op | source)
XLA Modules:
  0.0 4536.4 jit_solution(195619505325914754)
XLA Ops:
  17.4 42.8 all-reduce.19
  60.9 66.4 %all-gather = bf16[32,1,256]{2,1,0:T(2,128)(2,1)S(1)} all-gather(bf16[1,1,256]{2,1,0:T(2,128)(2,1)S(1)} %reshape.225), channel_id=1, replica_groups=mesh['dp'=8,'ctx'=4] {'dp','ctx'}, dimensions={0}, use_global_device_ids=true | all-gather | bytes 16896 | tf_op jit(solution)/shard_map/all_gather | solution.py:110
  128.1 1.2 convert_reduce_fusion.1
  129.3 1.3 fusion.42
  131.5 1.8 fusion.38
  133.3 16.1 all_gather.54
  149.4 4.7 fusion.14
  155.8 1.4 copy-done
  157.2 0.9 fusion.27
  158.2 70.7 %all-gather.11.cloned.1.call-done = bf16[2048,2048]{1,0:T(8,128)(2,1)} async-done(((bf16[64,2048]{1,0:T(8,128)(2,1)}), bf16[2048,2048]{1,0:T(8,128)(2,1)}) %all-gather.11.cloned.1.call-update) | async-done | bytes 8388624 | tf_op jit(solution)/shard_map/all_gather | solution.py:52
  228.9 4.7 fusion.77
  233.9 191.2 %all-gather.13.cloned.1.call-done = bf16[2048,8192]{1,0:T(8,128)(2,1)} async-done(((bf16[64,8192]{1,0:T(8,128)(2,1)}), bf16[2048,8192]{1,0:T(8,128)(2,1)}) %all-gather.13.cloned.1.call-update) | async-done | bytes 33554448 | tf_op jit(solution)/shard_map/all_gather | solution.py:109
  425.1 18.0 convolution_add_fusion
  443.1 177.8 %all-gather.15.cloned.1.call-done = bf16[8192,2048]{1,0:T(8,128)(2,1)} async-done(((bf16[256,2048]{1,0:T(8,128)(2,1)}), bf16[8192,2048]{1,0:T(8,128)(2,1)}) %all-gather.15.cloned.1.call-update) | async-done | bytes 33554448 | tf_op jit(solution)/shard_map/all_gather | solution.py:111
  620.8 20.1 convert_reduce_fusion
  641.0 19.8 multiply_reduce_fusion
  660.8 1.6 fusion.75
  664.0 7.1 convolution_convert_fusion
  671.1 2.0 copy.65
  673.2 3.3 fusion.7
  678.6 1.9 convert_reduce_fusion.4
  682.3 7.5 fusion.78
  689.7 10.5 reduce-scatter.19.cloned.1.call-done
  700.2 2.8 fusion.73
  703.0 1.1 fusion.41
  704.1 2.0 convert_reduce_fusion.2
  706.9 1.9 fusion.69
  709.1 8.2 fusion.51
  717.4 1.0 copy-done.5
  718.5 8.0 fusion.79
  726.6 24.9 fusion.68
  751.9 25.5 fusion.53
  778.0 17.7 fusion.16
  795.8 36.1 all-reduce.22.cloned.1.call-done
  831.9 1.3 dynamic-slice.1
  833.2 1.3 dynamic-slice.2
  834.4 1.3 dynamic-slice.3
  835.7 1.3 dynamic-slice.5
  836.9 1.3 dynamic-slice.6
  838.2 1.3 dynamic-slice.7
  839.5 1.3 dynamic-slice.9
  840.7 1.2 dynamic-slice.4
  841.9 1.3 dynamic-slice.8
  843.2 130.9 %reduce-scatter.11.cloned.1.call-done = f32[64,256]{1,0:T(8,128)} async-done(((f32[2048,256]{1,0:T(8,128)}), f32[64,256]{1,0:T(8,128)}) %reduce-scatter.11.cloned.1.call-update) | async-done | bytes 65552 | tf_op jit(solution)/shard_map/reduce_scatter | solution.py:233
  974.2 364.9 %reduce-scatter.9.cloned.1.call-done = f32[64,2048]{1,0:T(8,128)} async-done(((f32[2048,2048]{1,0:T(8,128)}), f32[64,2048]{1,0:T(8,128)}) %reduce-scatter.9.cloned.1.call-update) | async-done | bytes 524304 | tf_op jit(solution)/shard_map/reduce_scatter | solution.py:231
  1339.1 365.0 %reduce-scatter.13.cloned.1.call-done = f32[64,2048]{1,0:T(8,128)} async-done(((f32[2048,2048]{1,0:T(8,128)}), f32[64,2048]{1,0:T(8,128)}) %reduce-scatter.13.cloned.1.call-update) | async-done | bytes 524304 | tf_op jit(solution)/shard_map/reduce_scatter | solution.py:235
  1704.1 1411.7 %reduce-scatter.15.cloned.1.call-done = f32[64,8192]{1,0:T(8,128)} async-done(((f32[2048,8192]{1,0:T(8,128)}), f32[64,8192]{1,0:T(8,128)}) %reduce-scatter.15.cloned.1.call-update) | async-done | bytes 2097168 | tf_op jit(solution)/shard_map/reduce_scatter | solution.py:163
  3115.8 1413.5 %reduce-scatter.17.cloned.1.call-done = f32[256,2048]{1,0:T(8,128)} async-done(((f32[8192,2048]{1,0:T(8,128)}), f32[256,2048]{1,0:T(8,128)}) %reduce-scatter.17.cloned.1.call-update) | async-done | bytes 2097168 | tf_op jit(solution)/shard_map/reduce_scatter | solution.py:147
  (104 shorter events, 22.1 us)
Async XLA Ops:
  7.2 142.2 %copy-start.2 = (bf16[1,128,2048]{2,1,0:T(8,128)(2,1)S(1)}, bf16[1,128,2048]{2,1,0:T(8,128)(2,1)}, u32[]{:S(2)}) copy-start(bf16[1,128,2048]{2,1,0:T(8,128)(2,1)} %param.17) | copy-start | bytes 1572868
  7.2 124.3 %all-gather.7.cloned.1.call-start = ((), (), s32[]{:S(2)}) async-start(), calls=%async_computation.6 | async-start | bytes 1081344 | tf_op jit(solution)/shard_map/all_gather | solution.py:50
  7.9 141.5 %all-gather.9.cloned.1.call-start = ((), (), s32[]{:S(2)}) async-start(), calls=%async_computation.7 | async-start | bytes 8650752 | tf_op jit(solution)/shard_map/all_gather | solution.py:48
  8.7 220.2 %all-gather.11.cloned.1.call-start = ((), (), s32[]{:S(2)}) async-start(), calls=%async_computation.8 | async-start | bytes 8650752 | tf_op jit(solution)/shard_map/all_gather | solution.py:52
  9.4 415.7 %all-gather.13.cloned.1.call-start = ((), (), s32[]{:S(2)}) async-start(), calls=%async_computation.9 | async-start | bytes 34603008 | tf_op jit(solution)/shard_map/all_gather | solution.py:109
  10.0 610.9 %all-gather.15.cloned.1.call-start = ((), (), s32[]{:S(2)}) async-start(), calls=%async_computation.10 | async-start | bytes 34603008 | tf_op jit(solution)/shard_map/all_gather | solution.py:111
  10.6 689.7 %reduce-scatter.19.cloned.1.call-start = ((), (), s32[]{:S(2)}) async-start(), calls=%async_computation.16 | async-start | bytes 327680
  154.4 1.4 copy-start.10
  155.2 2.0 copy-start
  158.2 75.4 %copy-start.8 = (bf16[128,16,128]{2,0,1:T(8,128)(2,1)}, bf16[128,16,128]{2,0,1:T(8,128)(2,1)S(1)}, u32[]{:S(2)}) copy-start(bf16[128,16,128]{2,0,1:T(8,128)(2,1)S(1)} %fusion.27) | copy-start | bytes 1572868
  425.1 195.8 %copy-start.3 = (bf16[1,128,2048]{2,1,0:T(8,128)(2,1)S(1)}, bf16[1,128,2048]{2,1,0:T(8,128)(2,1)}, u32[]{:S(2)}) copy-start(bf16[1,128,2048]{2,1,0:T(8,128)(2,1)} %param.33) | copy-start | bytes 1572868
  663.2 0.8 copy-start.4
  673.1 3.6 copy-start.1
  673.2 3.7 copy-start.6
  677.7 2.8 copy-start.11
  682.2 149.7 %all-reduce.22.cloned.1.call-start = ((), (), s32[]{:S(2)}) async-start(), calls=%async_computation.17 | async-start | bytes 181248
  700.2 5.9 slice-start
  700.2 6.7 copy-start.12
  706.1 3.1 copy-start.7
  706.9 267.3 %reduce-scatter.11.cloned.1.call-start = ((), (), s32[]{:S(2)}) async-start(), calls=%async_computation.12 | async-start | bytes 2162688 | tf_op jit(solution)/shard_map/reduce_scatter | solution.py:233
  708.9 630.2 %reduce-scatter.9.cloned.1.call-start = ((), (), s32[]{:S(2)}) async-start(), calls=%async_computation.11 | async-start | bytes 17301504 | tf_op jit(solution)/shard_map/reduce_scatter | solution.py:231
  717.3 1.0 copy-start.5
  717.3 1.2 copy-start.9
  717.3 986.7 %reduce-scatter.13.cloned.1.call-start = ((), (), s32[]{:S(2)}) async-start(), calls=%async_computation.13 | async-start | bytes 17301504 | tf_op jit(solution)/shard_map/reduce_scatter | solution.py:235
  726.6 2389.2 %reduce-scatter.15.cloned.1.call-start = ((), (), s32[]{:S(2)}) async-start(), calls=%async_computation.14 | async-start | bytes 69206016 | tf_op jit(solution)/shard_map/reduce_scatter | solution.py:163
  751.6 3777.7 %reduce-scatter.17.cloned.1.call-start = ((), (), s32[]{:S(2)}) async-start(), calls=%async_computation.15 | async-start | bytes 69206016 | tf_op jit(solution)/shard_map/reduce_scatter | solution.py:147
  777.4 0.7 copy-start.13
Sparse Core Ops, SparseCore 0:
  11.0 56.6 all-gather.6
  70.7 78.4 all-gather.8
  152.1 76.7 all-gather.10
  231.6 193.3 all-gather.12
  427.8 192.9 all-gather.14
  682.3 17.8 reduce-scatter.18
  708.4 123.4 all-reduce.21
  834.7 139.4 reduce-scatter.10
  977.2 361.8 reduce-scatter.8
  1341.9 362.1 reduce-scatter.12
  1707.1 1408.5 reduce-scatter.14
  3118.7 1410.5 reduce-scatter.16
where the time goes:
time: 4540 us
  waiting for transfers between devices  4180 us (92%)
  matrix products  181 us (4%)
  blocking collectives  125 us (3%)
    reduce_scatter x1, waiting for transfers between devices, local(): lax.psum_scatter(grad_weight_down, ('dp', 'ctx'), scatter_dimension=0, ti...  1410 us
    reduce_scatter x1, waiting for transfers between devices, local(): lax.psum_scatter(grad_weight_up, ('dp', 'ctx'), scatter_dimension=0, tile...  1410 us
    reduce_scatter x1, waiting for transfers between devices, local(): lax.psum_scatter(grad_weight_out, ('dp', 'ctx'), scatter_dimension=0, til...  365 us
    reduce_scatter x1, waiting for transfers between devices, local(): lax.psum_scatter(grad_weight_query, ('dp', 'ctx'), scatter_dimension=0, t...  365 us
    all_gather x1, waiting for transfers between devices, local(): lax.all_gather(up_weight, ('dp', 'ctx'), axis=0, tiled=True)  191 us
    all_gather x1, waiting for transfers between devices, local(): lax.all_gather(down_weight, ('dp', 'ctx'), axis=0, tiled=True)  178 us
    reduce_scatter x1, waiting for transfers between devices, local(): lax.psum_scatter(grad_weight_kv, ('dp', 'ctx'), scatter_dimension=0, tile...  131 us
  transfers between devices with their start and end apart: 12, of which 10 were waited for; matrix products, arithmetic and copies ran while one was open for 3% of the time, Pallas kernels for 0%

commit v1 on v0

--- a/solution.py
+++ b/solution.py
@@ -6,6 +6,18 @@
 HEADS = 16
 HD = 128
 epsilon = 1e-05
+
+
+def doubled_up(x, axis, dim):
+    ways, here, step = (lax.axis_size(axis), lax.axis_index(axis), x.shape[dim])
+    line, have = (x, 1)
+    while have < ways:
+        line = jnp.concatenate(
+            [line, lax.ppermute(line, axis, [(d, (d - have) % ways) for d in range(ways)])],
+            axis=dim,
+        )
+        have = 2 * have
+    return jnp.roll(line, here * step, axis=dim)
 
 
 def norm_rows(values, gain, shift):
@@ -108,7 +120,7 @@
         lax.all_gather(ln2_bias, ("dp", "ctx"), axis=0, tiled=True),
         lax.all_gather(up_weight, ("dp", "ctx"), axis=0, tiled=True),
         lax.all_gather(up_bias, ("dp", "ctx"), axis=0, tiled=True),
-        lax.all_gather(down_weight, ("dp", "ctx"), axis=0, tiled=True),
+        doubled_up(down_weight, ("dp", "ctx"), 0),
         lax.all_gather(down_bias, ("dp", "ctx"), axis=0, tiled=True),
     )
     gain_two, shift_two, weight_up, bias_up, weight_down, bias_down = mlp_full

time: 4540 us -> 4610 us (1.015)
  local copies, waits for them, and re-layouts: 27.1 us -> 89 us
    ppermute x0 -> x5, waiting for transfers between devices: none -> 855 us  [doubled_up(): lax.ppermute(line, axis, [(d, (d - have) % ways) for d in range(ways)])]
    reduce_scatter x1, waiting for transfers between devices: 365 us -> 0.01 us  [local(): lax.psum_scatter(grad_weight_query, ('dp', 'ctx'), scatter_dimension=0, t...]
    reduce_scatter x1, waiting for transfers between devices: 365 us -> 41.9 us  [local(): lax.psum_scatter(grad_weight_out, ('dp', 'ctx'), scatter_dimension=0, til...]
    reduce_scatter x1, waiting for transfers between devices: 131 us -> 0.01 us  [local(): lax.psum_scatter(grad_weight_kv, ('dp', 'ctx'), scatter_dimension=0, tile...]
  transfers between devices with their start and end apart: 12 -> 17, of which waited for: 10 -> 12; matrix products, arithmetic and copies ran while one was open for 3% -> 5% of each run, Pallas kernels for 0% -> 0%
where the time goes in v1:
time: 4610 us; the launch traced here: 4600 us
  waiting for transfers between devices  4180 us (91%)
  matrix products  179 us (4%)
  blocking collectives  125 us (3%)
  local copies, waits for them, and re-layouts  89 us (2%)
    reduce_scatter x1, waiting for transfers between devices, local(): lax.psum_scatter(grad_weight_down, ('dp', 'ctx'), scatter_dimension=0, ti...  1410 us
    reduce_scatter x1, waiting for transfers between devices, local(): lax.psum_scatter(grad_weight_up, ('dp', 'ctx'), scatter_dimension=0, tile...  1410 us
    ppermute x5, waiting for transfers between devices, doubled_up(): lax.ppermute(line, axis, [(d, (d - have) % ways) for d in range(ways)])  855 us
    all_gather x1, waiting for transfers between devices, local(): lax.all_gather(up_weight, ('dp', 'ctx'), axis=0, tiled=True)  191 us
    all_gather x1, waiting for transfers between devices, local(): lax.all_gather(down_weight, ('dp', 'ctx'), axis=0, tiled=True)  178 us
  transfers between devices with their start and end apart: 17, of which 12 were waited for; matrix products, arithmetic and copies ran while one was open for 5% of the time, Pallas kernels for 0%

profile of v1, /device:TPU:0, one launch (start us, length us, event | category | flops | bytes accessed | tf_op | source)
XLA Modules:
  0.0 4604.5 jit_solution(2856173056942458078)
XLA Ops:
  17.4 42.8 all-reduce.19
  60.9 66.4 %all-gather = bf16[32,1,256]{2,1,0:T(2,128)(2,1)S(1)} all-gather(bf16[1,1,256]{2,1,0:T(2,128)(2,1)S(1)} %reshape.225), channel_id=1, replica_groups=mesh['dp'=8,'ctx'=4] {'dp','ctx'}, dimensions={0}, use_global_device_ids=true | all-gather | bytes 16896 | tf_op jit(solution)/shard_map/all_gather | solution.py:122
  131.4 1.8 fusion.49
  133.3 16.1 all_gather.53
  149.4 4.7 fusion.24
  155.7 1.4 copy-done
  158.0 70.8 %all-gather.11.cloned.1.call-done = bf16[2048,2048]{1,0:T(8,128)(2,1)} async-done(((bf16[64,2048]{1,0:T(8,128)(2,1)}), bf16[2048,2048]{1,0:T(8,128)(2,1)}) %all-gather.11.cloned.1.call-update) | async-done | bytes 8388624 | tf_op jit(solution)/shard_map/all_gather | solution.py:64
  228.8 4.7 fusion.89
  233.9 191.2 %all-gather.13.cloned.1.call-done = bf16[2048,8192]{1,0:T(8,128)(2,1)} async-done(((bf16[64,8192]{1,0:T(8,128)(2,1)}), bf16[2048,8192]{1,0:T(8,128)(2,1)}) %all-gather.13.cloned.1.call-update) | async-done | bytes 33554448 | tf_op jit(solution)/shard_map/all_gather | solution.py:121
  425.0 18.0 convolution_add_fusion
  443.0 177.8 %all-gather.15.cloned.1.call-done = bf16[8192,2048]{1,0:T(8,128)(2,1)} async-done(((bf16[256,2048]{1,0:T(8,128)(2,1)}), bf16[8192,2048]{1,0:T(8,128)(2,1)}) %all-gather.15.cloned.1.call-update) | async-done | bytes 33554448 | tf_op jit(solution)/shard_map/all_gather | solution.py:146
  620.8 19.7 convert_reduce_fusion
  640.5 19.8 multiply_reduce_fusion
  660.4 1.6 fusion.87
  663.7 7.1 convolution_convert_fusion
  670.8 2.0 copy.65
  672.8 3.3 fusion.9
  679.3 1.9 convert_reduce_fusion.4
  682.1 7.5 fusion.90
  689.5 10.5 reduce-scatter.19.cloned.1.call-done
  700.0 2.8 fusion.85
  703.9 2.0 convert_reduce_fusion.2
  706.7 1.9 fusion.81
  709.0 8.3 fusion.62
  718.5 8.1 fusion.91
  726.6 24.9 fusion.80
  751.6 25.5 fusion.64
  778.6 23.6 collective-permute-done
  802.5 96.2 %collective-permute-done.1 = bf16[512,2048]{1,0:T(8,128)(2,1)S(1)} collective-permute-done((bf16[512,2048]{1,0:T(8,128)(2,1)S(1)}, bf16[512,2048]{1,0:T(8,128)(2,1)S(1)}, u32[]{:S(2)}, u32[]{:S(2)}) %collective-permute-start.1) | collective-permute-done | bytes 2097184 | tf_op jit(solution)/shard_map/ppermute | solution.py:16
  899.3 1.3 collective-permute-start.2
  900.7 49.9 %collective-permute-done.2 = bf16[1024,2048]{1,0:T(8,128)(2,1)S(1)} collective-permute-done((bf16[1024,2048]{1,0:T(8,128)(2,1)S(1)}, bf16[1024,2048]{1,0:T(8,128)(2,1)S(1)}, u32[]{:S(2)}, u32[]{:S(2)}) %collective-permute-start.2) | collective-permute-done | bytes 4194336 | tf_op jit(solution)/shard_map/ppermute | solution.py:16
  950.6 4.5 pad_maximum_fusion
  956.4 1.6 constant_dynamic-update-slice_fusion.4
  957.9 1.6 constant_dynamic-update-slice_fusion.3
  959.5 2.5 constant_dynamic-update-slice_fusion.2
  962.1 4.3 constant_dynamic-update-slice_fusion.1
  966.4 209.4 %collective-permute-done.3 = bf16[2048,2048]{1,0:T(8,128)(2,1)S(1)} collective-permute-done((bf16[2048,2048]{1,0:T(8,128)(2,1)}, bf16[2048,2048]{1,0:T(8,128)(2,1)S(1)}, u32[]{:S(2)}, u32[]{:S(2)}) %collective-permute-start.3) | collective-permute-done | bytes 8388640 | tf_op jit(solution)/shard_map/ppermute | solution.py:16
  1175.8 7.2 constant_dynamic-update-slice_fusion
  1184.1 476.1 %collective-permute-done.4 = bf16[4096,2048]{1,0:T(8,128)(2,1)} collective-permute-done((bf16[4096,2048]{1,0:T(8,128)(2,1)}, bf16[4096,2048]{1,0:T(8,128)(2,1)}, u32[]{:S(2)}, u32[]{:S(2)}) %collective-permute-start.4) | collective-permute-done | bytes 16777248 | tf_op jit(solution)/shard_map/ppermute | solution.py:16
  1660.2 14.5 constant_dynamic-update-slice_fusion.11
  1676.9 1.5 constant_dynamic-update-slice_fusion.8
  1678.4 2.2 constant_dynamic-update-slice_fusion.7
  1680.7 8.3 constant_dynamic-update-slice_fusion.6
  1688.9 14.2 constant_dynamic-update-slice_fusion.5
  1703.1 15.7 fusion.25
  1730.1 41.9 reduce-scatter.13.cloned.1.call-done
  1772.0 1411.6 %reduce-scatter.15.cloned.1.call-done = f32[64,8192]{1,0:T(8,128)} async-done(((f32[2048,8192]{1,0:T(8,128)}), f32[64,8192]{1,0:T(8,128)}) %reduce-scatter.15.cloned.1.call-update) | async-done | bytes 2097168 | tf_op jit(solution)/shard_map/reduce_scatter | solution.py:175
  3183.6 1413.5 %reduce-scatter.17.cloned.1.call-done = f32[256,2048]{1,0:T(8,128)} async-done(((f32[8192,2048]{1,0:T(8,128)}), f32[256,2048]{1,0:T(8,128)}) %reduce-scatter.17.cloned.1.call-update) | async-done | bytes 2097168 | tf_op jit(solution)/shard_map/reduce_scatter | solution.py:159
  (145 shorter events, 45.0 us)
Async XLA Ops:
  7.2 142.2 %copy-start.5 = (bf16[1,128,2048]{2,1,0:T(8,128)(2,1)S(1)}, bf16[1,128,2048]{2,1,0:T(8,128)(2,1)}, u32[]{:S(2)}) copy-start(bf16[1,128,2048]{2,1,0:T(8,128)(2,1)} %param.17) | copy-start | bytes 1572868
  7.2 124.2 %all-gather.7.cloned.1.call-start = ((), (), s32[]{:S(2)}) async-start(), calls=%async_computation.6 | async-start | bytes 1081344 | tf_op jit(solution)/shard_map/all_gather | solution.py:62
  7.9 141.4 %all-gather.9.cloned.1.call-start = ((), (), s32[]{:S(2)}) async-start(), calls=%async_computation.7 | async-start | bytes 8650752 | tf_op jit(solution)/shard_map/all_gather | solution.py:60
  8.7 220.2 %all-gather.11.cloned.1.call-start = ((), (), s32[]{:S(2)}) async-start(), calls=%async_computation.8 | async-start | bytes 8650752 | tf_op jit(solution)/shard_map/all_gather | solution.py:64
  9.4 415.6 %all-gather.13.cloned.1.call-start = ((), (), s32[]{:S(2)}) async-start(), calls=%async_computation.9 | async-start | bytes 34603008 | tf_op jit(solution)/shard_map/all_gather | solution.py:121
  10.0 610.8 %all-gather.15.cloned.1.call-start = ((), (), s32[]{:S(2)}) async-start(), calls=%async_computation.10 | async-start | bytes 34603008 | tf_op jit(solution)/shard_map/all_gather | solution.py:146
  10.6 689.5 %reduce-scatter.19.cloned.1.call-start = ((), (), s32[]{:S(2)}) async-start(), calls=%async_computation.16 | async-start | bytes 327680
  154.3 1.4 copy-start.18
  155.1 2.0 copy-start
  158.0 75.6 %copy-start.16 = (bf16[128,16,128]{2,0,1:T(8,128)(2,1)}, bf16[128,16,128]{2,0,1:T(8,128)(2,1)S(1)}, u32[]{:S(2)}) copy-start(bf16[128,16,128]{2,0,1:T(8,128)(2,1)S(1)} %fusion.38) | copy-start | bytes 1572868
  425.0 195.8 %copy-start.11 = (bf16[1,128,2048]{2,1,0:T(8,128)(2,1)S(1)}, bf16[1,128,2048]{2,1,0:T(8,128)(2,1)}, u32[]{:S(2)}) copy-start(bf16[1,128,2048]{2,1,0:T(8,128)(2,1)} %param.33) | copy-start | bytes 1572868
  662.8 0.8 copy-start.12
  672.8 3.6 copy-start.1
  672.8 3.7 copy-start.14
  677.4 1.0 copy-start.19
  682.0 1036.7 %all-reduce.22.cloned.1.call-start = ((), (), s32[]{:S(2)}) async-start(), calls=%async_computation.17 | async-start | bytes 181248
  700.0 5.9 slice-start
  700.0 6.7 copy-start.20
  705.9 3.1 copy-start.15
  706.7 1023.5 %reduce-scatter.11.cloned.1.call-start = ((), (), s32[]{:S(2)}) async-start(), calls=%async_computation.12 | async-start | bytes 2162688 | tf_op jit(solution)/shard_map/reduce_scatter | solution.py:245
  708.7 1021.5 %reduce-scatter.9.cloned.1.call-start = ((), (), s32[]{:S(2)}) async-start(), calls=%async_computation.11 | async-start | bytes 17301504 | tf_op jit(solution)/shard_map/reduce_scatter | solution.py:243
  717.3 1.0 copy-start.13
  717.3 1.2 copy-start.17
  717.3 1054.7 %reduce-scatter.13.cloned.1.call-start = ((), (), s32[]{:S(2)}) async-start(), calls=%async_computation.13 | async-start | bytes 17301504 | tf_op jit(solution)/shard_map/reduce_scatter | solution.py:247
  726.6 2457.0 %reduce-scatter.15.cloned.1.call-start = ((), (), s32[]{:S(2)}) async-start(), calls=%async_computation.14 | async-start | bytes 69206016 | tf_op jit(solution)/shard_map/reduce_scatter | solution.py:175
  751.6 3845.6 %reduce-scatter.17.cloned.1.call-start = ((), (), s32[]{:S(2)}) async-start(), calls=%async_computation.15 | async-start | bytes 69206016 | tf_op jit(solution)/shard_map/reduce_scatter | solution.py:159
  777.1 1.2 copy-start.4
  778.4 23.8 collective-permute-start
  802.2 155.8 %copy-start.9 = (bf16[256,2048]{1,0:T(8,128)(2,1)}, bf16[256,2048]{1,0:T(8,128)(2,1)S(1)}, u32[]{:S(2)}) copy-start(bf16[256,2048]{1,0:T(8,128)(2,1)S(1)} %collective-permute-done) | copy-start | bytes 3145732
  802.4 96.3 %collective-permute-start.1 = (bf16[512,2048]{1,0:T(8,128)(2,1)S(1)}, bf16[512,2048]{1,0:T(8,128)(2,1)S(1)}, u32[]{:S(2)}, u32[]{:S(2)}) collective-permute-start(bf16[512,2048]{1,0:T(8,128)(2,1)S(1)} %pad_maximum_fusion.2), channel_id=1, source_target_pairs={{0,30},{1,31},{2,0},{3,1},{4,2},{5,3},{6,4},{7,5},{8,6},{9,7},{10,... | collective-permute-start | bytes 6291464 | tf_op jit(solution)/shard_map/ppermute | solution.py:16
  898.7 60.9 %copy-start.7 = (bf16[512,2048]{1,0:T(8,128)(2,1)}, bf16[512,2048]{1,0:T(8,128)(2,1)S(1)}, u32[]{:S(2)}) copy-start(bf16[512,2048]{1,0:T(8,128)(2,1)S(1)} %collective-permute-done.1) | copy-start | bytes 6291460
  899.3 51.3 %collective-permute-start.2 = (bf16[1024,2048]{1,0:T(8,128)(2,1)S(1)}, bf16[1024,2048]{1,0:T(8,128)(2,1)S(1)}, u32[]{:S(2)}, u32[]{:S(2)}) collective-permute-start(bf16[1024,2048]{1,0:T(8,128)(2,1)S(1)} %pad_maximum_fusion.1), channel_id=1, source_target_pairs={{0,28},{1,29},{2,30},{3,31},{4,0},{5,1},{6,2},{7,3},{8,4},{9,5},{1... | collective-permute-start | bytes 12582920 | tf_op jit(solution)/shard_map/ppermute | solution.py:16
  950.6 11.5 copy-start.2
  955.2 220.7 %collective-permute-start.3 = (bf16[2048,2048]{1,0:T(8,128)(2,1)}, bf16[2048,2048]{1,0:T(8,128)(2,1)S(1)}, u32[]{:S(2)}, u32[]{:S(2)}) collective-permute-start(bf16[2048,2048]{1,0:T(8,128)(2,1)} %pad_maximum_fusion), channel_id=1, source_target_pairs={{0,24},{1,25},{2,26},{3,27},{4,28},{5,29},{6,30},{7,31},{8,0},{9,1... | collective-permute-start | bytes 25165832 | tf_op jit(solution)/shard_map/ppermute | solution.py:16
  1175.8 8.3 copy-start.6
  1175.8 8.3 copy-start.21
  1184.1 476.2 %collective-permute-start.4 = (bf16[4096,2048]{1,0:T(8,128)(2,1)}, bf16[4096,2048]{1,0:T(8,128)(2,1)}, u32[]{:S(2)}, u32[]{:S(2)}) collective-permute-start(bf16[4096,2048]{1,0:T(8,128)(2,1)} %get-tuple-element.44), channel_id=1, source_target_pairs={{0,16},{1,17},{2,18},{3,19},{4,20},{5,21},{6,22},{7,23},{8,24},{9,... | collective-permute-start | bytes 50331656 | tf_op jit(solution)/shard_map/ppermute | solution.py:16
  1660.2 15.6 copy-start.10
  1660.2 16.7 copy-start.8
  1674.8 3.6 copy-start.3
Sparse Core Ops, SparseCore 0:
  11.0 56.6 all-gather.6
  70.7 78.3 all-gather.8
  152.0 76.8 all-gather.10
  231.6 193.3 all-gather.12
  427.8 192.9 all-gather.14
  682.1 17.8 reduce-scatter.18
  708.2 162.9 all-reduce.21
  874.0 168.9 reduce-scatter.10
  1046.0 360.9 reduce-scatter.8
  1409.8 362.1 reduce-scatter.12
  1775.1 1408.5 reduce-scatter.14
  3186.5 1410.5 reduce-scatter.16
